TPU v7x, 256 devices: a whole 4x4x8 slice. The times are simulated.
256 devices in a mesh: grp: 8 (over y, z_hi), tp: 4 (over z_lo), ffn: 8 (over x, core).
Axes of the slice: x: 4, y: 4, z: 8 (z_hi: 2, z_lo: 4; z = z_hi * 4 + z_lo), core: 2. Of those that a mesh axis runs over, the one named last changes fastest.
Arguments:
- queries: bfloat16 [768, 8192], P('grp', 'tp'), may hold values from -320 to 320
- new_kv: bfloat16 [2, 768, 1024], P(None, 'grp', 'tp'), may hold values from -12 to 12
- kv_cache: bfloat16 [2, 8, 16384, 1024], P(None, 'grp', 'ffn', 'tp'), may hold values from -12 to 12
- lengths: int32 [8], P('grp'), may hold values from 1 to 96, as said below
- prefixes: int32 [8], P('grp'), may hold values from 0 to 16384, as said below
- resid: bfloat16 [768, 8192], P('grp', 'ffn'), may hold values from -0.29882812 to 0.29882812
- out_weight: bfloat16 [8192, 8192], P('tp', 'ffn'), may hold values from -0.0625 to 0.0625
- gain: bfloat16 [8192], P('ffn'), may hold values from 0.099609375 to 1.8984375
- gate_weight: bfloat16 [8192, 29568], P('ffn', ('grp', 'tp')), may hold values from -0.0625 to 0.0625
- up_weight: bfloat16 [8192, 29568], P('ffn', ('grp', 'tp')), may hold values from -0.0625 to 0.0625
- down_weight: bfloat16 [29568, 8192], P(('grp', 'tp'), 'ffn'), may hold values from -0.03125 to 0.03125
Outputs:
- layer_out: bfloat16 [768, 8192], P(('grp', 'tp'), 'ffn')
Inputs may be any that keep to these rules, and one draw needn't show every extreme that they name: `lengths`: some group has a full block of 96 live slots. `prefixes`: some group has all 16384 cached positions in use.
All inputs are finite; a program needn't handle non-finite values.
Results may differ from a plain program's by a relative error of at most 0.02.
Values may be sent and summed in bfloat16 or wider, within the bound.
A program may use at most 64 MiB of HBM per device.

v0:
```python
import math
import jax
import jax.numpy as jnp
from jax import lax
from jax.sharding import PartitionSpec as P

D = 8192
DH = 128
negative = -1e30


def merged(x, axis, combine):
    everything = jax.tree.map(lambda part: lax.all_gather(part, axis), x)
    leading = jax.tree.map(lambda part: part[0], everything)

    def hop(k, so_far):
        return combine(so_far, jax.tree.map(lambda part: part[k], everything))

    return lax.fori_loop(1, lax.axis_size(axis), hop, leading)


def combine_parts(first, second):
    top = jnp.maximum(first[0], second[0])
    left = jnp.exp(first[0] - top)
    right = jnp.exp(second[0] - top)
    total = first[1] * left + second[1] * right
    values = first[2] * left[..., None] + second[2] * right[..., None]
    return (top, total, values)


def body(
    queries,
    new_kv,
    kv_cache,
    lengths,
    prefixes,
    resid,
    out_weight,
    gain,
    gate_weight,
    up_weight,
    down_weight,
):
    span, qcols = queries.shape
    kcols = new_kv.shape[2]
    local_kv = kcols // DH
    group = qcols // DH // local_kv
    cache_len = kv_cache.shape[2]
    length = lengths[0]
    prefix = prefixes[0]
    width_index = lax.axis_index("ffn")
    shard_start = width_index * cache_len
    query_heads = (
        queries.reshape(span, local_kv, group, DH)
        .transpose(1, 2, 0, 3)
        .reshape(local_kv, group * span, DH)
    )
    row_pos = jnp.tile(jnp.arange(span, dtype=jnp.int32), group)
    inv_scale = 1.0 / math.sqrt(DH)

    def update(state, keys, values, valid):
        top, total, acc = state
        scores = (
            jnp.einsum("hrd,hkd->hrk", query_heads, keys, preferred_element_type=jnp.float32)
            * inv_scale
        )
        scores = jnp.where(valid[None], scores, negative)
        new_top = jnp.maximum(top, jnp.max(scores, axis=-1))
        probs = jnp.where(valid[None], jnp.exp(scores - new_top[..., None]), 0.0)
        factor = jnp.exp(top - new_top)
        total = total * factor + jnp.sum(probs, axis=-1)
        acc = acc * factor[..., None] + jnp.einsum(
            "hrk,hkd->hrd", probs, values.astype(jnp.float32)
        )
        return (new_top, total, acc)

    block = math.gcd(512, cache_len)
    blocks = cache_len // block
    cache_keys = kv_cache[0, 0].reshape(blocks, block, local_kv, DH).transpose(0, 2, 1, 3)
    cache_values = kv_cache[1, 0].reshape(blocks, block, local_kv, DH).transpose(0, 2, 1, 3)
    rows = group * span
    start_state = (
        jnp.full((local_kv, rows), negative, jnp.float32),
        jnp.zeros((local_kv, rows), jnp.float32),
        jnp.zeros((local_kv, rows, DH), jnp.float32),
    )

    def cache_step(state, items):
        keys, values, index = items
        positions = shard_start + index * block + jnp.arange(block, dtype=jnp.int32)
        valid = jnp.broadcast_to((positions < prefix)[None, :], (rows, block))
        return (update(state, keys, values, valid), None)

    state, unused = lax.scan(
        cache_step, start_state, (cache_keys, cache_values, jnp.arange(blocks, dtype=jnp.int32))
    )
    block_keys = new_kv[0].reshape(span, local_kv, DH).transpose(1, 0, 2)
    block_values = new_kv[1].reshape(span, local_kv, DH).transpose(1, 0, 2)
    slots = jnp.arange(span, dtype=jnp.int32)[None, :]
    new_valid = (slots < length) & (slots <= row_pos[:, None]) & (width_index == 0)
    state = update(state, block_keys, block_values, new_valid)
    top, total, acc = merged(state, "ffn", combine_parts)
    heads = acc / total[..., None]
    attn = (
        heads.reshape(local_kv, group, span, DH)
        .transpose(2, 0, 1, 3)
        .reshape(span, qcols)
        .astype(jnp.bfloat16)
    )
    partial_value = jnp.dot(attn, out_weight, preferred_element_type=jnp.float32)
    summed = lax.psum(partial_value, "tp")
    h1 = (summed + resid.astype(jnp.float32)).astype(jnp.bfloat16)
    all_rows = lax.all_gather(h1, "grp", axis=0, tiled=True)
    rows_f = all_rows.astype(jnp.float32)
    squares = jnp.sum(rows_f * rows_f, axis=1)
    scaled = (rows_f * gain.astype(jnp.float32)[None, :]).astype(jnp.bfloat16)
    gate = jnp.dot(scaled, gate_weight, preferred_element_type=jnp.float32)
    upper = jnp.dot(scaled, up_weight, preferred_element_type=jnp.float32)
    rows_here = span // lax.axis_size("tp")
    gate, upper, squares = lax.psum((gate, upper, squares), "ffn")
    inv_rms = lax.rsqrt(squares / D + 1e-06)
    hidden = (jax.nn.silu(gate * inv_rms[:, None]) * (upper * inv_rms[:, None])).astype(
        jnp.bfloat16
    )
    down_rows = lax.psum_scatter(
        jnp.dot(hidden, down_weight, preferred_element_type=jnp.float32),
        ("grp", "tp"),
        scatter_dimension=0,
        tiled=True,
    )
    row_start = lax.axis_index("tp") * rows_here
    own = lax.dynamic_slice_in_dim(h1, row_start, rows_here, 0)
    live = row_start + jnp.arange(rows_here, dtype=jnp.int32) < length
    return jnp.where(live[:, None], own.astype(jnp.float32) + down_rows, 0.0).astype(jnp.bfloat16)


def solution(mesh):
    return jax.shard_map(
        body,
        mesh=mesh,
        in_specs=(
            P("grp", "tp"),
            P(None, "grp", "tp"),
            P(None, "grp", "ffn", "tp"),
            P("grp"),
            P("grp"),
            P("grp", "ffn"),
            P("tp", "ffn"),
            P("ffn"),
            P("ffn", ("grp", "tp")),
            P("ffn", ("grp", "tp")),
            P(("grp", "tp"), "ffn"),
        ),
        out_specs=P(("grp", "tp"), "ffn"),
        check_vma=False,
    )
```

profile of v0, /device:TPU:2, one launch (start us, length us, event | category | flops | bytes accessed | tf_op | source)
XLA Modules:
  0.0 559.2 jit_solution(7451356754690004521)
XLA Ops:
  7.4 0.8 fusion.48
  8.3 1.1 copy.31
  9.5 3.0 fusion.47
  12.5 1.3 reshape_squeeze.13
  13.9 2.1 reshape_squeeze.12
  16.0 28.8 %while.35 = (s32[]{:T(128)}, f32[2,768]{1,0:T(2,128)S(1)}, f32[2,768]{1,0:T(2,128)S(1)}, f32[2,768,128]{2,1,0:T(8,128)}, s32[4]{0:T(128)S(1)}, /*index=5*/s32[]{...) while((s32[]{:T(128)}, f32[2,768]{1,0:T(2,128)S(1)}, ...), condition=%wide.region_3.4_spmd.clone, body=%wide.region_0.3_spmd.clone.sunk | while | flops 412688896 | bytes 19368184 | solution.py:94
  16.0 0.6 dynamic_slice.64
  17.3 0.7 add_compare_fusion.3
  17.9 1.3 constant_dynamic-slice_fusion.3
  19.3 0.6 bitcast_reduce_fusion.2
  19.9 0.9 fusion.69
  20.8 1.5 fusion.71
  22.4 0.9 copy-done.3
  23.2 0.6 dynamic_slice.64
  24.5 0.7 add_compare_fusion.3
  25.1 1.3 constant_dynamic-slice_fusion.3
  26.5 0.6 bitcast_reduce_fusion.2
  27.1 0.9 fusion.69
  28.0 1.5 fusion.71
  29.6 0.9 copy-done.3
  30.4 0.6 dynamic_slice.64
  31.7 0.7 add_compare_fusion.3
  32.3 1.3 constant_dynamic-slice_fusion.3
  33.7 0.6 bitcast_reduce_fusion.2
  34.3 0.9 fusion.69
  35.2 1.5 fusion.71
  36.8 0.9 copy-done.3
  37.6 0.6 dynamic_slice.64
  38.9 0.7 add_compare_fusion.3
  39.5 1.3 constant_dynamic-slice_fusion.3
  40.9 0.6 bitcast_reduce_fusion.2
  41.5 0.9 fusion.69
  42.4 1.5 fusion.71
  44.0 0.9 copy-done.3
  44.8 0.1 fusion.38
  44.9 0.3 fusion.49
  45.2 0.1 fusion.31
  45.4 2.5 convolution_add_fusion
  48.0 12.9 %all-gather.4 = f32[8,2,768]{2,1,0:T(2,128)S(1)} all-gather(f32[1,2,768]{2,1,0:T(2,128)S(1)} %get-tuple-element.336), channel_id=3, replica_groups=mesh['grp'=8,'tp'=4,'ffn'=8] {'ffn'}, dimensions={0}, use_global_device_ids=true | all-gather | bytes 55296 | tf_op jit(solution)/shard_map/all_gather | solution.py:13
  60.8 12.8 %all-gather.3 = f32[8,2,768]{2,1,0:T(2,128)S(1)} all-gather(f32[1,2,768]{2,1,0:T(2,128)S(1)} %bitcast.107), channel_id=2, replica_groups=mesh['grp'=8,'tp'=4,'ffn'=8] {'ffn'}, dimensions={0}, use_global_device_ids=true | all-gather | bytes 55296 | tf_op jit(solution)/shard_map/all_gather | solution.py:13
  73.6 20.0 %all-gather.10.cloned.1.call-done = f32[16,768,128]{2,1,0:T(8,128)} async-done(((f32[2,768,128]{2,1,0:T(8,128)}), f32[16,768,128]{2,1,0:T(8,128)}) %all-gather.10.cloned.1.call-update) | async-done | bytes 6291472 | tf_op jit(solution)/shard_map/all_gather | solution.py:13
  93.6 1.2 slice.35
  94.8 13.0 %while.34 = (s32[]{:T(128)}, f32[2,768]{1,0:T(2,128)S(1)}, f32[2,768]{1,0:T(2,128)S(1)}, f32[2,768,128]{2,1,0:T(8,128)S(1)}, f32[8,2,768]{2,1,0:T(2,128)S(1)}, /...) while((s32[]{:T(128)}, f32[2,768]{1,0:T(2,128)S(1)}, ...), condition=%wide.region_7.8_spmd, body=%wide.region_6.7_spmd.sunk | while | flops 599045 | bytes 2420879 | solution.py:19
  94.9 1.8 fusion.65
  96.7 1.8 fusion.65
  98.6 1.8 fusion.65
  100.5 1.8 fusion.65
  102.3 1.8 fusion.65
  104.2 1.8 fusion.65
  106.0 1.8 fusion.65
  107.8 0.3 divide_convert_fusion
  108.1 0.2 copy.27
  108.3 3.8 fusion.32
  112.2 52.0 %all-reduce.4.cloned.1.call-done = f32[96,1024]{1,0:T(8,128)} async-done(((f32[96,1024]{1,0:T(8,128)}), f32[96,1024]{1,0:T(8,128)}) %all-reduce.4.cloned.1.call-update) | async-done | bytes 393232 | tf_op jit(solution)/shard_map/psum | solution.py:111
  164.2 1.7 add_convert_fusion
  165.9 69.0 %all-gather.8.cloned.1.call-done = bf16[768,1024]{1,0:T(8,128)(2,1)} async-done(((bf16[96,1024]{1,0:T(8,128)(2,1)}), bf16[768,1024]{1,0:T(8,128)(2,1)}) %all-gather.8.cloned.1.call-update) | async-done | bytes 1572880 | tf_op jit(solution)/shard_map/all_gather | solution.py:113
  235.0 5.4 fusion.26
  240.4 3.3 fusion.28
  243.7 0.4 fusion.24
  244.1 10.0 %psum.30 = f32[768]{0:T(1024)S(1)} all-reduce(f32[768]{0:T(1024)S(1)} %fusion.24), channel_id=1, replica_groups=mesh['grp'=8,'tp'=4,'ffn'=8] {'ffn'}, use_global_device_ids=true, to_apply=%region_11.12 | all-reduce | flops 768 | bytes 6144 | tf_op jit(solution)/shard_map/psum | solution.py:120
  254.2 68.5 %all-reduce.6.cloned.1.call-done = (f32[768,924]{0,1:T(8,128)}, f32[768,924]{0,1:T(8,128)}) async-done(((f32[768,924]{0,1:T(8,128)}, f32[768,924]{0,1:T(8,128)}), (f32[768,924]{0,1:T(8,128)}, f32[768,924]{0,1:T(8,128)})) %all-reduce.6.cloned.1.call-update) | async-done | bytes 5677072 | tf_op jit(solution)/shard_map/psum | solution.py:120
  322.7 6.2 %fusion.25 = f32[768,1024]{1,0:T(8,128)} fusion(bf16[924,1024]{1,0:T(8,128)(2,1)S(1)} %copy-done, f32[768,924]{0,1:T(8,128)} %get-tuple-element.328, f32[768,924]{0,1:T(8,128)} %get-tuple-element.329, f32[768]{0:T(1024)S(1)} %add_rsqrt_fusion), kind=kOutput, calls=%fused_computation.42 | convolution fusion | flops 1459003392 | bytes 10718208 | tf_op jit(solution)/shard_map/dot_general | solution.py:126
  329.0 222.1 %reduce-scatter.2.cloned.1.call-done = f32[24,1024]{1,0:T(8,128)} async-done(((f32[768,1024]{1,0:T(8,128)}), f32[24,1024]{1,0:T(8,128)}) %reduce-scatter.2.cloned.1.call-update) | async-done | bytes 98320 | tf_op jit(solution)/shard_map/reduce_scatter | solution.py:125
  551.1 1.6 select_convert_fusion
  (68 shorter events, 0.9 us)
Async XLA Ops:
  6.5 316.1 %copy-start = (bf16[924,1024]{1,0:T(8,128)(2,1)S(1)}, bf16[924,1024]{1,0:T(8,128)(2,1)}, u32[]{:S(2)}) copy-start(bf16[924,1024]{1,0:T(8,128)(2,1)} %param.25) | copy-start | bytes 5677060
  6.5 87.1 %all-gather.10.cloned.1.call-start = ((), (), s32[]{:S(2)}) async-start(), calls=%async_computation.4 | async-start | bytes 7077888 | tf_op jit(solution)/shard_map/all_gather | solution.py:13
  19.3 1.5 copy-start.2
  22.3 0.9 copy-start.3
  26.5 1.5 copy-start.2
  29.5 0.9 copy-start.3
  33.7 1.5 copy-start.2
  36.7 0.9 copy-start.3
  40.9 1.5 copy-start.2
  43.9 0.9 copy-start.3
  47.9 116.2 %all-reduce.4.cloned.1.call-start = ((), (), s32[]{:S(2)}) async-start(), calls=%async_computation.1 | async-start | bytes 786432 | tf_op jit(solution)/shard_map/psum | solution.py:111
  108.3 55.9 %copy-start.4 = (bf16[96,1024]{1,0:T(8,128)(2,1)S(1)}, bf16[96,1024]{1,0:T(8,128)(2,1)}, u32[]{:S(2)}) copy-start(bf16[96,1024]{1,0:T(8,128)(2,1)} %param.20) | copy-start | bytes 589828
  108.3 57.6 %copy-start.5 = (bf16[1024]{0:T(1024)(128)(2,1)S(1)}, bf16[1024]{0:T(1024)(128)(2,1)}, u32[]{:S(2)}) copy-start(bf16[1024]{0:T(1024)(128)(2,1)} %param.22) | copy-start | bytes 6148
  112.1 122.8 %all-gather.8.cloned.1.call-start = ((), (), s32[]{:S(2)}) async-start(), calls=%async_computation.2 | async-start | bytes 1769472 | tf_op jit(solution)/shard_map/all_gather | solution.py:113
  165.9 156.8 %all-reduce.6.cloned.1.call-start = ((), (), s32[]{:S(2)}) async-start(), calls=%async_computation.5 | async-start | bytes 11403264 | tf_op jit(solution)/shard_map/psum | solution.py:120
  235.0 5.4 copy-start.1
  235.0 5.4 copy-start.6
  243.7 307.4 %reduce-scatter.2.cloned.1.call-start = ((), (), s32[]{:S(2)}) async-start(), calls=%async_computation.3 | async-start | bytes 3244032 | tf_op jit(solution)/shard_map/reduce_scatter | solution.py:125
Sparse Core Ops, SparseCore 0:
  48.0 45.5 all-gather.9
  112.2 51.8 all-reduce.3
  167.1 67.8 all-gather.7
  243.8 78.8 all-reduce.5
  329.1 221.9 reduce-scatter.1
where the time goes:
time: 560 us; the launch traced here: 559 us
  waiting for transfers between devices  432 us (77%)
  blocking collectives  35.7 us (6%)
  matrix products  30 us (5%)
  other arithmetic  23.3 us (4%)
  local copies, waits for them, and re-layouts  21.3 us (4%)
  between operations  14.1 us (3%)
    reduce_scatter x1, waiting for transfers between devices, body(): lax.psum_scatter(jnp.dot(hidden, down_weight, preferred_element_type=jnp....  222 us
    all_gather x1, waiting for transfers between devices, body(): all_rows = lax.all_gather(h1, 'grp', axis=0, tiled=True)  69 us
    psum x1, waiting for transfers between devices, body(): gate, upper, squares = lax.psum((gate, upper, squares), 'ffn')  68.5 us
    psum x1, waiting for transfers between devices, body(): summed = lax.psum(partial_value, 'tp')  52 us
    all_gather x2, blocking collectives, merged(): everything = jax.tree.map(lambda part: lax.all_gather(part, axis), x)  25.6 us
    all_gather x1, waiting for transfers between devices, merged(): everything = jax.tree.map(lambda part: lax.all_gather(part, axis), x)  20 us
    add x7, other arithmetic, combine_parts(): values = first[2] * left[..., None] + second[2] * right[..., None]  12.6 us
  transfers between devices with their start and end apart: 5, of which 5 were waited for; matrix products, arithmetic and copies ran while one was open for 0% of the time, Pallas kernels for 0%

commit v1 on v0

--- a/solution.py
+++ b/solution.py
@@ -110,7 +110,9 @@
     partial_value = jnp.dot(attn, out_weight, preferred_element_type=jnp.float32)
     summed = lax.psum(partial_value, "tp")
     h1 = (summed + resid.astype(jnp.float32)).astype(jnp.bfloat16)
-    all_rows = lax.all_gather(h1, "grp", axis=0, tiled=True)
+    all_rows = jnp.concatenate(
+        lax.all_to_all(jnp.stack([h1] * lax.axis_size("grp")), "grp", 0, 0), axis=0
+    )
     rows_f = all_rows.astype(jnp.float32)
     squares = jnp.sum(rows_f * rows_f, axis=1)
     scaled = (rows_f * gain.astype(jnp.float32)[None, :]).astype(jnp.bfloat16)

time: 560 us -> 538 us (0.961)
  waiting for transfers between devices: 432 us -> 402 us
  starting transfers between devices: 0.17 us -> 6.94 us
    all_gather x1 -> x0, waiting for transfers between devices: 69 us -> none  [body(): all_rows = lax.all_gather(h1, 'grp', axis=0, tiled=True)]
    all_to_all x0 -> x1, waiting for transfers between devices: none -> 35.1 us  [body(): lax.all_to_all(jnp.stack([h1] * lax.axis_size('grp')), 'grp', 0, 0)]
    all_to_all x0 -> x1, starting transfers between devices: none -> 6.81 us  [body(): lax.all_to_all(jnp.stack([h1] * lax.axis_size('grp')), 'grp', 0, 0)]
where the time goes in v1:
time: 538 us; the launch traced here: 537 us
  waiting for transfers between devices  402 us (75%)
  blocking collectives  35.6 us (7%)
  matrix products  27.8 us (5%)
  local copies, waits for them, and re-layouts  24.5 us (5%)
  other arithmetic  23 us (4%)
  between operations  14.1 us (3%)
  starting transfers between devices  6.94 us (1%)
    reduce_scatter x1, waiting for transfers between devices, body(): lax.psum_scatter(jnp.dot(hidden, down_weight, preferred_element_type=jnp....  222 us
    psum x1, waiting for transfers between devices, body(): gate, upper, squares = lax.psum((gate, upper, squares), 'ffn')  72.6 us
    psum x1, waiting for transfers between devices, body(): summed = lax.psum(partial_value, 'tp')  52 us
    all_to_all x1, waiting for transfers between devices, body(): lax.all_to_all(jnp.stack([h1] * lax.axis_size('grp')), 'grp', 0, 0)  35.1 us
    all_gather x2, blocking collectives, merged(): everything = jax.tree.map(lambda part: lax.all_gather(part, axis), x)  25.6 us
    all_gather x1, waiting for transfers between devices, merged(): everything = jax.tree.map(lambda part: lax.all_gather(part, axis), x)  20 us
    add x7, other arithmetic, combine_parts(): values = first[2] * left[..., None] + second[2] * right[..., None]  12.6 us
  transfers between devices with their start and end apart: 5, of which 5 were waited for; matrix products, arithmetic and copies ran while one was open for 0% of the time, Pallas kernels for 0%

profile of v1, /device:TPU:2, one launch (start us, length us, event | category | flops | bytes accessed | tf_op | source)
XLA Modules:
  0.0 536.7 jit_solution(15967455581443982343)
XLA Ops:
  7.4 0.8 fusion.43
  8.3 1.1 copy.38
  9.5 3.0 fusion.42
  12.5 1.3 reshape_squeeze.13
  13.9 2.1 reshape_squeeze.12
  16.0 28.8 %while.35 = (s32[]{:T(128)}, f32[2,768]{1,0:T(2,128)S(1)}, f32[2,768]{1,0:T(2,128)S(1)}, f32[2,768,128]{2,1,0:T(8,128)}, s32[4]{0:T(128)S(1)}, /*index=5*/s32[]{...) while((s32[]{:T(128)}, f32[2,768]{1,0:T(2,128)S(1)}, ...), condition=%wide.region_3.4_spmd.clone, body=%wide.region_0.3_spmd.clone.sunk | while | flops 412688896 | bytes 19368184 | solution.py:94
  16.0 0.6 dynamic_slice.64
  17.3 0.7 add_compare_fusion.3
  17.9 1.3 constant_dynamic-slice_fusion.3
  19.3 0.6 bitcast_reduce_fusion.2
  19.9 0.9 fusion.68
  20.8 1.5 fusion.70
  22.4 0.9 copy-done.3
  23.2 0.6 dynamic_slice.64
  24.5 0.7 add_compare_fusion.3
  25.1 1.3 constant_dynamic-slice_fusion.3
  26.5 0.6 bitcast_reduce_fusion.2
  27.1 0.9 fusion.68
  28.0 1.5 fusion.70
  29.6 0.9 copy-done.3
  30.4 0.6 dynamic_slice.64
  31.7 0.7 add_compare_fusion.3
  32.3 1.3 constant_dynamic-slice_fusion.3
  33.7 0.6 bitcast_reduce_fusion.2
  34.3 0.9 fusion.68
  35.2 1.5 fusion.70
  36.8 0.9 copy-done.3
  37.6 0.6 dynamic_slice.64
  38.9 0.7 add_compare_fusion.3
  39.5 1.3 constant_dynamic-slice_fusion.3
  40.9 0.6 bitcast_reduce_fusion.2
  41.5 0.9 fusion.68
  42.4 1.5 fusion.70
  44.0 0.9 copy-done.3
  45.4 2.5 convolution_add_fusion
  48.0 12.9 %all-gather.4 = f32[8,2,768]{2,1,0:T(2,128)S(1)} all-gather(f32[1,2,768]{2,1,0:T(2,128)S(1)} %get-tuple-element.346), channel_id=3, replica_groups=mesh['grp'=8,'tp'=4,'ffn'=8] {'ffn'}, dimensions={0}, use_global_device_ids=true | all-gather | bytes 55296 | tf_op jit(solution)/shard_map/all_gather | solution.py:13
  60.8 12.8 %all-gather.3 = f32[8,2,768]{2,1,0:T(2,128)S(1)} all-gather(f32[1,2,768]{2,1,0:T(2,128)S(1)} %bitcast.113), channel_id=2, replica_groups=mesh['grp'=8,'tp'=4,'ffn'=8] {'ffn'}, dimensions={0}, use_global_device_ids=true | all-gather | bytes 55296 | tf_op jit(solution)/shard_map/all_gather | solution.py:13
  73.6 20.0 %all-gather.7.cloned.1.call-done = f32[16,768,128]{2,1,0:T(8,128)} async-done(((f32[2,768,128]{2,1,0:T(8,128)}), f32[16,768,128]{2,1,0:T(8,128)}) %all-gather.7.cloned.1.call-update) | async-done | bytes 6291472 | tf_op jit(solution)/shard_map/all_gather | solution.py:13
  93.6 1.2 slice.35
  94.8 13.0 %while.34 = (s32[]{:T(128)}, f32[2,768]{1,0:T(2,128)S(1)}, f32[2,768]{1,0:T(2,128)S(1)}, f32[2,768,128]{2,1,0:T(8,128)S(1)}, f32[8,2,768]{2,1,0:T(2,128)S(1)}, /...) while((s32[]{:T(128)}, f32[2,768]{1,0:T(2,128)S(1)}, ...), condition=%wide.region_7.8_spmd, body=%wide.region_6.7_spmd.sunk | while | flops 599045 | bytes 2420879 | solution.py:19
  94.9 1.8 fusion.64
  96.7 1.8 fusion.64
  98.6 1.8 fusion.64
  100.5 1.8 fusion.64
  102.3 1.8 fusion.64
  104.2 1.8 fusion.64
  106.0 1.8 fusion.64
  108.3 3.8 fusion.27
  112.1 52.0 %all-reduce.4.cloned.1.call-done = f32[96,1024]{1,0:T(8,128)} async-done(((f32[96,1024]{1,0:T(8,128)}), f32[96,1024]{1,0:T(8,128)}) %all-reduce.4.cloned.1.call-update) | async-done | bytes 393232 | tf_op jit(solution)/shard_map/psum | solution.py:111
  164.1 1.0 add_convert_fusion
  165.2 0.7 copy-done.1
  165.8 1.3 stack.2
  167.2 6.8 %all-to-all-start = ((bf16[8,96,1024]{2,1,0:T(8,128)(2,1)}), bf16[8,96,1024]{2,1,0:T(8,128)(2,1)S(1)}, u32[]{:S(2)}, u32[]{:S(2)}) async-start(bf16[8,96,1024]{2,1,0:T(8,128)(2,1)} %stack.2), calls=%async_computation | async-start | bytes 3145728 | tf_op jit(solution)/shard_map/all_to_all | solution.py:114
  174.1 35.1 %all-to-all-done = bf16[8,96,1024]{2,1,0:T(8,128)(2,1)S(1)} async-done(((bf16[8,96,1024]{2,1,0:T(8,128)(2,1)}), bf16[8,96,1024]{2,1,0:T(8,128)(2,1)S(1)}, u32[]{:S(2)}, u32[]{:S(2)}) %all-to-all-start) | async-done | bytes 1572896 | tf_op jit(solution)/shard_map/all_to_all | solution.py:114
  209.1 0.4 fusion.23
  209.5 1.1 copy-done.6
  210.7 3.2 fusion.46
  213.9 3.3 fusion.45
  217.3 0.4 multiply_reduce_fusion
  217.7 10.0 %psum.30 = f32[768]{0:T(1024)S(1)} all-reduce(f32[768]{0:T(1024)S(1)} %reduce_sum.31), channel_id=1, replica_groups=mesh['grp'=8,'tp'=4,'ffn'=8] {'ffn'}, use_global_device_ids=true, to_apply=%region_11.12 | all-reduce | flops 768 | bytes 6144 | tf_op jit(solution)/shard_map/psum | solution.py:122
  227.7 72.6 %all-reduce.6.cloned.1.call-done = (f32[768,924]{0,1:T(8,128)}, f32[768,924]{0,1:T(8,128)}) async-done(((f32[768,924]{0,1:T(8,128)}, f32[768,924]{0,1:T(8,128)}), (f32[768,924]{0,1:T(8,128)}, f32[768,924]{0,1:T(8,128)})) %all-reduce.6.cloned.1.call-update) | async-done | bytes 5677072 | tf_op jit(solution)/shard_map/psum | solution.py:122
  300.4 6.2 %fusion.24 = f32[768,1024]{1,0:T(8,128)} fusion(bf16[924,1024]{1,0:T(8,128)(2,1)S(1)} %copy-done, f32[768,924]{0,1:T(8,128)} %get-tuple-element.338, f32[768,924]{0,1:T(8,128)} %get-tuple-element.339, f32[768]{0:T(1024)S(1)} %add_rsqrt_fusion), kind=kOutput, calls=%fused_computation.41 | convolution fusion | flops 1459003392 | bytes 10718208 | tf_op jit(solution)/shard_map/dot_general | solution.py:128
  306.7 221.9 %reduce-scatter.2.cloned.1.call-done = f32[24,1024]{1,0:T(8,128)} async-done(((f32[768,1024]{1,0:T(8,128)}), f32[24,1024]{1,0:T(8,128)}) %reduce-scatter.2.cloned.1.call-update) | async-done | bytes 98320 | tf_op jit(solution)/shard_map/reduce_scatter | solution.py:127
  528.6 1.6 select_convert_fusion
  (72 shorter events, 1.9 us)
Async XLA Ops:
  6.5 293.8 %copy-start = (bf16[924,1024]{1,0:T(8,128)(2,1)S(1)}, bf16[924,1024]{1,0:T(8,128)(2,1)}, u32[]{:S(2)}) copy-start(bf16[924,1024]{1,0:T(8,128)(2,1)} %param.25) | copy-start | bytes 5677060
  6.5 87.1 %all-gather.7.cloned.1.call-start = ((), (), s32[]{:S(2)}) async-start(), calls=%async_computation.4 | async-start | bytes 7077888 | tf_op jit(solution)/shard_map/all_gather | solution.py:13
  19.3 1.5 copy-start.2
  22.3 0.9 copy-start.3
  26.5 1.5 copy-start.2
  29.5 0.9 copy-start.3
  33.7 1.5 copy-start.2
  36.7 0.9 copy-start.3
  40.9 1.5 copy-start.2
  43.9 0.9 copy-start.3
  47.9 116.2 %all-reduce.4.cloned.1.call-start = ((), (), s32[]{:S(2)}) async-start(), calls=%async_computation.2 | async-start | bytes 786432 | tf_op jit(solution)/shard_map/psum | solution.py:111
  108.3 55.9 %copy-start.4 = (bf16[96,1024]{1,0:T(8,128)(2,1)S(1)}, bf16[96,1024]{1,0:T(8,128)(2,1)}, u32[]{:S(2)}) copy-start(bf16[96,1024]{1,0:T(8,128)(2,1)} %param.20) | copy-start | bytes 589828
  112.1 61.9 %copy-start.5 = (bf16[1024]{0:T(1024)(128)(2,1)S(1)}, bf16[1024]{0:T(1024)(128)(2,1)}, u32[]{:S(2)}) copy-start(bf16[1024]{0:T(1024)(128)(2,1)} %param.22) | copy-start | bytes 6148
  165.2 0.7 copy-start.1
  167.2 41.9 %all-to-all-start = ((bf16[8,96,1024]{2,1,0:T(8,128)(2,1)}), bf16[8,96,1024]{2,1,0:T(8,128)(2,1)S(1)}, u32[]{:S(2)}, u32[]{:S(2)}) async-start(bf16[8,96,1024]{2,1,0:T(8,128)(2,1)} %stack.2), calls=%async_computation | async-start | bytes 3145728 | tf_op jit(solution)/shard_map/all_to_all | solution.py:114
  174.0 126.4 %all-reduce.6.cloned.1.call-start = ((), (), s32[]{:S(2)}) async-start(), calls=%async_computation.5 | async-start | bytes 11403264 | tf_op jit(solution)/shard_map/psum | solution.py:122
  209.1 1.5 copy-start.6
  210.7 3.2 copy-start.7
  217.2 311.4 %reduce-scatter.2.cloned.1.call-start = ((), (), s32[]{:S(2)}) async-start(), calls=%async_computation.3 | async-start | bytes 3244032 | tf_op jit(solution)/shard_map/reduce_scatter | solution.py:127
Sparse Core Ops, SparseCore 0:
  48.0 45.5 all-gather.6
  112.2 51.8 all-reduce.3
  217.3 82.9 all-reduce.5
  306.8 221.7 reduce-scatter.1
